TPU v7x, 128 devices: a whole 4x4x4 slice. The times are simulated.
128 devices in a mesh: row: 8 (over x, y_hi), col: 16 (over y_lo, z, core).
Axes of the slice: x: 4, y: 4 (y_hi: 2, y_lo: 2; y = y_hi * 2 + y_lo), z: 4, core: 2. Of those that a mesh axis runs over, the one named last changes fastest.
Arguments:
- train_inputs: bfloat16 [512, 8192], P(('row', 'col')), may hold values from -6 to 6
- train_grads: bfloat16 [512, 8192], P(('row', 'col')), may hold values from -6 to 6
- query_inputs: bfloat16 [256, 8192], P(('row', 'col')), may hold values from -6 to 6
- query_grads: bfloat16 [256, 8192], P(('row', 'col')), may hold values from -6 to 6
- input_basis: bfloat16 [8192, 8192], P('row', 'col'), may hold values from -0.0625 to 0.0625
- output_basis: bfloat16 [8192, 8192], P('col', 'row'), may hold values from -0.0625 to 0.0625
- eigenvalues: float32 [8192, 8192], P('row', 'col'), may hold values from 0.5 to 5
- query_starts: int32 [16], replicated, may hold values from 0 to 255, as said below
- query_ends: int32 [16], replicated, may hold values from 1 to 256, as said below
Outputs:
- scores: float32 [16, 512], replicated
Inputs may be any that keep to these rules, and one draw needn't show every extreme that they name: Query q covers the query rows query_starts[q] <= r < query_ends[q]: a nonempty span of at most 128 rows that lies inside one aligned block of 128 rows (rows k * 128 to (k + 1) * 128 - 1); spans of different queries may intersect or share a block. `query_ends`: see query_starts.
All inputs are finite; a program needn't handle non-finite values.
Results may differ from a plain program's by a relative error of at most 0.005.
Values may be sent and summed in bfloat16 or wider, within the bound.
A program may use at most 64 MiB of HBM per device.

v0:
```python
import math
import jax
import jax.numpy as jnp
from jax import lax
from jax.sharding import Mesh
from jax.sharding import PartitionSpec as P

D_IN = 8192
D_OUT = 8192
QBLOCK = 128
COL = ("col_0", "col_1", "col_2")
ROW = ("row_0", "row_1")
ROW_COL = ("row_0", "row_1", "col_0", "col_1", "col_2")
damping = 0.1


def laid_out(parts, dim):
    parts = jnp.moveaxis(parts, 0, dim)
    dims = parts.shape
    return parts.reshape(*dims[:dim], dims[dim] * dims[dim + 1], *dims[dim + 2 :])


def gather_together(arrays, axis, dims):
    line = jnp.concatenate([a.reshape(-1) for a in arrays])
    lines, at, gathered = (lax.all_gather(line, axis), 0, [])
    for a, dim in zip(arrays, dims):
        parts = lines[:, at : at + a.size].reshape(-1, *a.shape)
        gathered.append(laid_out(parts, dim))
        at += a.size
    return tuple(gathered)


def by_axis(value, axes):
    for axis in axes:
        value = lax.psum(value, axis)
    return value


def shards(
    train_inputs,
    train_grads,
    query_inputs,
    query_grads,
    input_basis,
    output_basis,
    eigenvalues,
    query_starts,
    query_ends,
):
    grouped = gather_together((train_inputs, query_inputs), COL, (0, 0))
    train_in, query_in = (
        lax.all_to_all(grouped[0], ROW, split_axis=1, concat_axis=0, tiled=True),
        lax.all_to_all(grouped[1], ROW, split_axis=1, concat_axis=0, tiled=True),
    )
    spread = (
        lax.all_to_all(train_grads, COL, split_axis=1, concat_axis=0, tiled=True),
        lax.all_to_all(query_grads, COL, split_axis=1, concat_axis=0, tiled=True),
    )
    train_out, query_out = gather_together((spread[0], spread[1]), ROW, (0, 0))
    train_in_part = jnp.dot(train_in, input_basis, preferred_element_type=jnp.float32)
    query_in_part = jnp.dot(query_in, input_basis, preferred_element_type=jnp.float32)
    train_out_part = jnp.dot(train_out, output_basis, preferred_element_type=jnp.float32)
    query_out_part = jnp.dot(query_out, output_basis, preferred_element_type=jnp.float32)
    in_sums = lax.psum((train_in_part, query_in_part), ROW)
    out_sums = lax.psum((train_out_part, query_out_part), COL)
    train_in_rot = in_sums[0].astype(jnp.bfloat16)
    query_in_rot = in_sums[1].astype(jnp.bfloat16)
    train_grad_rot = out_sums[0].astype(jnp.bfloat16)
    query_grad_rot = out_sums[1].astype(jnp.bfloat16)
    grads_wide = train_grad_rot.astype(jnp.float32)
    denominator = eigenvalues + damping

    def per_query(span):
        span_start, span_end = span
        block_top = span_start // QBLOCK * QBLOCK
        grad_rows = lax.dynamic_slice_in_dim(query_grad_rot, block_top, QBLOCK, 0)
        input_rows = lax.dynamic_slice_in_dim(query_in_rot, block_top, QBLOCK, 0)
        positions = block_top + jnp.arange(QBLOCK, dtype=jnp.int32)
        inside = (positions >= span_start) & (positions < span_end)
        grad_rows = jnp.where(inside[:, None], grad_rows, jnp.zeros((), grad_rows.dtype))
        outer_sum = lax.dot_general(
            grad_rows, input_rows, (((0,), (0,)), ((), ())), preferred_element_type=jnp.float32
        )
        scaled = (outer_sum / denominator).astype(jnp.bfloat16)
        paired = lax.dot_general(
            train_in_rot, scaled, (((1,), (1,)), ((), ())), preferred_element_type=jnp.float32
        )
        return jnp.sum(grads_wide * paired, axis=1)

    partial_scores = lax.map(per_query, (query_starts, query_ends))
    totals = by_axis(partial_scores, ROW_COL)
    return totals * (1.0 / math.sqrt(D_IN * D_OUT * QBLOCK))


def solution(mesh):
    split = Mesh(mesh.devices.reshape(4, 2, 2, 4, 2), ("row_0", "row_1", "col_0", "col_1", "col_2"))
    placed = (
        P(ROW_COL, None),
        P(ROW_COL, None),
        P(ROW_COL, None),
        P(ROW_COL, None),
        P(ROW, COL),
        P(COL, ROW),
        P(ROW, COL),
        P(),
        P(),
    )
    return jax.shard_map(shards, mesh=split, in_specs=placed, out_specs=P(), check_vma=False)
```

profile of v0, /device:TPU:1, one launch (start us, length us, event | category | flops | bytes accessed | tf_op | source)
XLA Modules:
  0.0 458.6 jit_solution(13673715249605043826)
XLA Ops:
  8.9 13.6 %all_to_all.70 = bf16[2,16,512]{2,0,1:T(2,128)(2,1)S(1)} all-to-all(bf16[2,16,512]{2,0,1:T(2,128)(2,1)} %bitcast.54), channel_id=1, replica_groups=mesh['row_0'=4,'row_1'=2,'col_0'=2,'col_1'=4,'col_2'=2] {'col_0','col_1'..., dimensions={1} | all-to-all | bytes 65536 | tf_op jit(solution)/shard_map/all_to_all | solution.py:57
  22.6 3.7 all-to-all-start
  26.2 3.2 broadcast_add_fusion
  29.5 2.7 all-to-all-done
  32.2 31.4 %all-gather = bf16[393216]{0:T(1024)(128)(2,1)S(1)} all-gather(bf16[49152]{0:T(1024)(128)(2,1)S(1)} %pad_maximum_fusion), channel_id=2, replica_groups=mesh['row_0'=4,'row_1'=2,'col_0'=2,'col_1'=4,'col_2'=2] {'row_0','row_1'}, dimensions={0}, use_global_device_ids=true | all-gather | bytes 884736 | tf_op jit(solution)/shard_map/all_gather | solution.py:25
  65.0 1.8 reshape.40
  67.7 1.3 all_to_all.58
  70.1 4.5 all-to-all-start.2
  74.7 1.8 fusion.18
  77.3 2.5 fusion.15
  80.8 2.3 all_to_all.62
  83.1 2.8 copy.22
  85.9 6.6 %all-to-all-start.3 = ((bf16[64,8,1024]{2,0,1:T(8,128)(2,1)}), bf16[64,8,1024]{2,0,1:T(8,128)(2,1)}, u32[]{:S(2)}, u32[]{:S(2)}) async-start(bf16[64,8,1024]{2,0,1:T(8,128)(2,1)} %copy.22), calls=%async_computation.3 | async-start | bytes 2097152 | tf_op jit(solution)/shard_map/all_to_all | solution.py:52
  92.6 74.4 %all-reduce.4 = (bf16[256,1024]{1,0:T(8,128)(2,1)}, bf16[512,1024]{1,0:T(8,128)(2,1)}) all-reduce(f32[256,1024]{1,0:T(8,128)} %fusion.15, f32[512,1024]{1,0:T(8,128)S(1)} %fusion.18), channel_id=1, replica_groups=mesh['row_0'=4,'row_1'=2,'col_0'=2,'col_1'=4,'col_2'=2] {'col_0','col_1'..., use_global_device_ids=true, to_apply=%region_0.0 | all-reduce | flops 786432 | bytes 4718592 | tf_op jit(solution)/shard_map/psum | solution.py:65
  166.9 1.5 copy.23
  168.4 2.6 fusion.16
  171.0 3.3 fusion.17
  174.3 81.4 %all-reduce.5 = (bf16[256,512]{1,0:T(8,128)(2,1)}, bf16[512,512]{1,0:T(8,128)(2,1)}) all-reduce(f32[256,512]{1,0:T(8,128)} %fusion.16, f32[512,512]{1,0:T(8,128)} %fusion.17), channel_id=1, replica_groups=mesh['row_0'=4,'row_1'=2,'col_0'=2,'col_1'=4,'col_2'=2] {'row_0','row_1'}, use_global_device_ids=true, to_apply=%region_1.0 | all-reduce | flops 393216 | bytes 2359296 | tf_op jit(solution)/shard_map/psum | solution.py:64
  255.7 127.2 %while.12 = (s32[]{:T(128)}, f32[16,512]{1,0:T(8,128)S(1)}, s32[16]{0:T(128)S(1)}, s32[16]{0:T(128)S(1)}, bf16[256,1024]{1,0:T(8,128)(2,1)}, /*index=5*/bf16[256...) while((s32[]{:T(128)}, f32[16,512]{1,0:T(8,128)S(1)}, ...), condition=%wide.region_6.7_spmd, body=%wide.region_4.6_spmd.sunk | while | flops 673316864 | bytes 5119617 | solution.py:90
  259.4 1.2 compare_and_fusion.2
  260.6 2.9 fusion.35
  267.4 1.2 compare_and_fusion.2
  268.6 2.9 fusion.35
  275.3 1.2 compare_and_fusion.2
  276.6 2.9 fusion.35
  283.3 1.2 compare_and_fusion.2
  284.5 2.9 fusion.35
  291.2 1.2 compare_and_fusion.2
  292.5 2.9 fusion.35
  299.2 1.2 compare_and_fusion.2
  300.4 2.9 fusion.35
  307.1 1.2 compare_and_fusion.2
  308.4 2.9 fusion.35
  315.1 1.2 compare_and_fusion.2
  316.3 2.9 fusion.35
  324.3 2.9 fusion.35
  332.2 2.9 fusion.35
  340.2 2.9 fusion.35
  348.1 2.9 fusion.35
  356.1 2.9 fusion.35
  364.0 2.9 fusion.35
  372.0 2.9 fusion.35
  380.0 2.9 fusion.35
  383.0 11.8 %psum.67 = f32[16,512]{1,0:T(8,128)S(1)} all-reduce(f32[16,512]{1,0:T(8,128)S(1)} %get-tuple-element.119), channel_id=1, replica_groups=mesh['row_0'=4,'row_1'=2,'col_0'=2,'col_1'=4,'col_2'=2] {'row_0'}, use_global_device_ids=true, to_apply=%region_7.8 | all-reduce | flops 8192 | bytes 65536 | tf_op jit(solution)/shard_map/psum | solution.py:35
  394.8 7.5 %psum.68 = f32[16,512]{1,0:T(8,128)S(1)} all-reduce(f32[16,512]{1,0:T(8,128)S(1)} %psum.67), channel_id=1, replica_groups=mesh['row_0'=4,'row_1'=2,'col_0'=2,'col_1'=4,'col_2'=2] {'row_1'}, use_global_device_ids=true, to_apply=%region_8.9 | all-reduce | flops 8192 | bytes 65536 | tf_op jit(solution)/shard_map/psum | solution.py:35
  402.3 6.6 %psum.69 = f32[16,512]{1,0:T(8,128)S(1)} all-reduce(f32[16,512]{1,0:T(8,128)S(1)} %psum.68), channel_id=1, replica_groups=mesh['row_0'=4,'row_1'=2,'col_0'=2,'col_1'=4,'col_2'=2] {'col_0'}, use_global_device_ids=true, to_apply=%region_9.10 | all-reduce | flops 8192 | bytes 65536 | tf_op jit(solution)/shard_map/psum | solution.py:35
  409.0 18.8 %psum.70 = f32[16,512]{1,0:T(8,128)S(1)} all-reduce(f32[16,512]{1,0:T(8,128)S(1)} %psum.69), channel_id=1, replica_groups=mesh['row_0'=4,'row_1'=2,'col_0'=2,'col_1'=4,'col_2'=2] {'col_1'}, use_global_device_ids=true, to_apply=%region_10.11 | all-reduce | flops 8192 | bytes 65536 | tf_op jit(solution)/shard_map/psum | solution.py:35
  427.7 23.4 %psum.71 = f32[16,512]{1,0:T(8,128)S(1)} all-reduce(f32[16,512]{1,0:T(8,128)S(1)} %psum.70), channel_id=1, replica_groups=mesh['row_0'=4,'row_1'=2,'col_0'=2,'col_1'=4,'col_2'=2] {'col_2'}, use_global_device_ids=true, to_apply=%region_11.12 | all-reduce | flops 8192 | bytes 65536 | tf_op jit(solution)/shard_map/psum | solution.py:35
  (90 shorter events, 38.6 us)
Async XLA Ops:
  6.5 68.1 %copy-start = (bf16[512,1024]{1,0:T(8,128)(2,1)S(1)}, bf16[512,1024]{1,0:T(8,128)(2,1)}, u32[]{:S(2)}) copy-start(bf16[512,1024]{1,0:T(8,128)(2,1)} %param.16) | copy-start | bytes 3145732
  6.5 58.5 %all-gather.4.cloned.1.call-start = ((), (), s32[]{:S(2)}) async-start(), calls=%async_computation.4 | async-start | bytes 1671168 | tf_op jit(solution)/shard_map/all_gather | solution.py:25
  22.6 9.6 %all-to-all-start = ((bf16[4,16,512]{2,0,1:T(4,128)(2,1)}), bf16[4,16,512]{2,0,1:T(4,128)(2,1)S(1)}, u32[]{:S(2)}, u32[]{:S(2)}) async-start(bf16[4,16,512]{2,0,1:T(4,128)(2,1)} %bitcast.51), calls=%async_computation | async-start | bytes 131072 | tf_op jit(solution)/shard_map/all_to_all | solution.py:56
  63.9 1.1 copy-start.3
  66.8 3.3 copy-start.1
  70.1 6.3 %slice-start = ((bf16[8,49152]{1,0:T(8,128)(2,1)}), bf16[8,16384]{1,0:T(8,128)(2,1)S(1)}, s32[]{:S(2)}) async-start(bf16[8,49152]{1,0:T(8,128)(2,1)} %copy-done.3), calls=%async_computation.5 | async-start | bytes 524288 | tf_op jit(solution)/shard_map/slice | solution.py:27
  70.1 15.8 %all-to-all-start.2 = ((bf16[32,8,1024]{2,0,1:T(8,128)(2,1)}), bf16[32,8,1024]{2,0,1:T(8,128)(2,1)}, u32[]{:S(2)}, u32[]{:S(2)}) async-start(bf16[32,8,1024]{2,0,1:T(8,128)(2,1)} %copy.21), calls=%async_computation.2 | async-start | bytes 1048576 | tf_op jit(solution)/shard_map/all_to_all | solution.py:53
  77.2 2.5 copy-start.2
  85.9 85.1 %all-to-all-start.3 = ((bf16[64,8,1024]{2,0,1:T(8,128)(2,1)}), bf16[64,8,1024]{2,0,1:T(8,128)(2,1)}, u32[]{:S(2)}, u32[]{:S(2)}) async-start(bf16[64,8,1024]{2,0,1:T(8,128)(2,1)} %copy.22), calls=%async_computation.3 | async-start | bytes 2097152 | tf_op jit(solution)/shard_map/all_to_all | solution.py:52
  171.0 84.7 %copy-start.4 = (s32[16]{0:T(128)S(1)}, s32[16]{0:T(128)}, u32[]{:S(2)}) copy-start(s32[16]{0:T(128)} %param.18) | copy-start | bytes 196
  171.0 84.7 %copy-start.5 = (s32[16]{0:T(128)S(1)}, s32[16]{0:T(128)}, u32[]{:S(2)}) copy-start(s32[16]{0:T(128)} %param.19) | copy-start | bytes 196
Sparse Core Ops, SparseCore 0:
  9.1 38.4 all-gather.3
where the time goes:
time: 461 us; the launch traced here: 459 us
  blocking collectives  269 us (58%)
  matrix products  56.8 us (12%)
  loops' own time  40.5 us (9%)
  local copies, waits for them, and re-layouts  37.2 us (8%)
  other arithmetic  24.1 us (5%)
  starting transfers between devices  14.8 us (3%)
  between operations  13.5 us (3%)
    psum x1, blocking collectives, shards(): in_sums = lax.psum((train_in_part, query_in_part), ROW)  81.4 us
    psum x1, blocking collectives, shards(): out_sums = lax.psum((train_out_part, query_out_part), COL)  74.4 us
    psum x5, blocking collectives, by_axis(): value = lax.psum(value, axis)  68.1 us
    dot_general x16, matrix products, per_query(): lax.dot_general(train_in_rot, scaled, (((1,), (1,)), ((), ())), preferred...  46.7 us
    another operation x1, loops' own time, shards(): partial_scores = lax.map(per_query, (query_starts, query_ends))  40.5 us
    all_gather x1, blocking collectives, gather_together(): lines, at, gathered = (lax.all_gather(line, axis), 0, [])  31.4 us
    and x16, other arithmetic, per_query(): inside = (positions >= span_start) & (positions < span_end)  19.6 us
    dynamic_slice x32, local copies, waits for them, and re-layouts, shards(): partial_scores = lax.map(per_query, (query_starts, query_ends))  19.4 us
  transfers between devices with their start and end apart: 4, of which 1 were waited for; matrix products, arithmetic and copies ran while one was open for 4% of the time, Pallas kernels for 0%

commit v1 on v0

--- a/solution.py
+++ b/solution.py
@@ -4,6 +4,7 @@
 from jax import lax
 from jax.sharding import Mesh
 from jax.sharding import PartitionSpec as P
+from jax.lax import psum
 
 D_IN = 8192
 D_OUT = 8192
@@ -61,7 +62,9 @@
     query_in_part = jnp.dot(query_in, input_basis, preferred_element_type=jnp.float32)
     train_out_part = jnp.dot(train_out, output_basis, preferred_element_type=jnp.float32)
     query_out_part = jnp.dot(query_out, output_basis, preferred_element_type=jnp.float32)
-    in_sums = lax.psum((train_in_part, query_in_part), ROW)
+    in_sums = (train_in_part, query_in_part)
+    for j0 in ("row_0", "row_1"):
+        in_sums = psum(in_sums, j0)
     out_sums = lax.psum((train_out_part, query_out_part), COL)
     train_in_rot = in_sums[0].astype(jnp.bfloat16)
     query_in_rot = in_sums[1].astype(jnp.bfloat16)

time: 461 us -> 433 us (0.939)
  blocking collectives: 269 us -> 224 us
  waiting for transfers between devices: 2.68 us -> 23.1 us
    psum x1, blocking collectives: 81.4 us -> 37.6 us  [shards(): in_sums = psum(in_sums, j0)]
    all_gather x1, waiting for transfers between devices: 0.01 us -> 19.8 us  [gather_together(): lines, at, gathered = (lax.all_gather(line, axis), 0, [])]
    all_gather x1, blocking collectives: 31.4 us -> 39.5 us  [gather_together(): lines, at, gathered = (lax.all_gather(line, axis), 0, [])]
    psum x5, blocking collectives: 68.1 us -> 62.4 us  [by_axis(): value = lax.psum(value, axis)]
  transfers between devices with their start and end apart: 4 -> 5, of which waited for: 1 -> 2; matrix products, arithmetic and copies ran while one was open for 4% -> 5% of each run, Pallas kernels for 0% -> 0%
where the time goes in v1:
time: 433 us; the launch traced here: 431 us
  blocking collectives  224 us (52%)
  matrix products  56.6 us (13%)
  loops' own time  40.5 us (9%)
  local copies, waits for them, and re-layouts  35.1 us (8%)
  other arithmetic  24.1 us (6%)
  waiting for transfers between devices  23.1 us (5%)
  starting transfers between devices  14.1 us (3%)
  between operations  13.6 us (3%)
    psum x1, blocking collectives, shards(): out_sums = lax.psum((train_out_part, query_out_part), COL)  70.5 us
    psum x5, blocking collectives, by_axis(): value = lax.psum(value, axis)  62.4 us
    dot_general x16, matrix products, per_query(): lax.dot_general(train_in_rot, scaled, (((1,), (1,)), ((), ())), preferred...  46.7 us
    another operation x1, loops' own time, shards(): partial_scores = lax.map(per_query, (query_starts, query_ends))  40.5 us
    all_gather x1, blocking collectives, gather_together(): lines, at, gathered = (lax.all_gather(line, axis), 0, [])  39.5 us
    psum x1, blocking collectives, shards(): in_sums = psum(in_sums, j0)  37.6 us
    all_gather x1, waiting for transfers between devices, gather_together(): lines, at, gathered = (lax.all_gather(line, axis), 0, [])  19.8 us
    and x16, other arithmetic, per_query(): inside = (positions >= span_start) & (positions < span_end)  19.6 us
  transfers between devices with their start and end apart: 5, of which 2 were waited for; matrix products, arithmetic and copies ran while one was open for 5% of the time, Pallas kernels for 0%

profile of v1, /device:TPU:1, one launch (start us, length us, event | category | flops | bytes accessed | tf_op | source)
XLA Modules:
  0.0 430.6 jit_solution(11037794049871127775)
XLA Ops:
  8.9 13.6 %all_to_all.70 = bf16[2,16,512]{2,0,1:T(2,128)(2,1)S(1)} all-to-all(bf16[2,16,512]{2,0,1:T(2,128)(2,1)} %bitcast.55), channel_id=1, replica_groups=mesh['row_0'=4,'row_1'=2,'col_0'=2,'col_1'=4,'col_2'=2] {'col_0','col_1'..., dimensions={1} | all-to-all | bytes 65536 | tf_op jit(solution)/shard_map/all_to_all | solution.py:58
  22.6 3.7 all-to-all-start
  26.2 19.8 %all-gather.4.cloned.1.call-done = bf16[786432]{0:T(1024)(128)(2,1)} async-done(((bf16[49152]{0:T(1024)(128)(2,1)}), bf16[786432]{0:T(1024)(128)(2,1)}) %all-gather.4.cloned.1.call-update) | async-done | bytes 1572880 | tf_op jit(solution)/shard_map/all_gather | solution.py:26
  46.1 1.8 reshape.40
  48.7 1.3 all_to_all.58
  51.1 6.1 %all-to-all-start.2 = ((bf16[32,8,1024]{2,0,1:T(8,128)(2,1)}), bf16[32,8,1024]{2,0,1:T(8,128)(2,1)S(1)}, u32[]{:S(2)}, u32[]{:S(2)}) async-start(bf16[32,8,1024]{2,0,1:T(8,128)(2,1)} %copy.21), calls=%async_computation.2 | async-start | bytes 1048576 | tf_op jit(solution)/shard_map/all_to_all | solution.py:54
  57.2 3.2 broadcast_add_fusion
  61.5 1.6 all_to_all.62
  63.1 1.6 copy.22
  64.6 3.3 all-to-all-done.2
  67.9 4.2 all-to-all-start.3
  72.2 39.5 %all-gather = bf16[393216]{0:T(1024)(128)(2,1)S(1)} all-gather(bf16[49152]{0:T(1024)(128)(2,1)S(1)} %pad_maximum_fusion), channel_id=2, replica_groups=mesh['row_0'=4,'row_1'=2,'col_0'=2,'col_1'=4,'col_2'=2] {'row_0','row_1'}, dimensions={0}, use_global_device_ids=true | all-gather | bytes 884736 | tf_op jit(solution)/shard_map/all_gather | solution.py:26
  113.2 2.4 fusion.16
  115.6 3.2 fusion.17
  118.9 1.8 fusion.18
  121.5 2.4 fusion.15
  123.9 70.5 %all-reduce.9 = (bf16[256,1024]{1,0:T(8,128)(2,1)}, bf16[512,1024]{1,0:T(8,128)(2,1)}) all-reduce(f32[256,1024]{1,0:T(8,128)} %fusion.15, f32[512,1024]{1,0:T(8,128)S(1)} %fusion.18), channel_id=1, replica_groups=mesh['row_0'=4,'row_1'=2,'col_0'=2,'col_1'=4,'col_2'=2] {'col_0','col_1'..., use_global_device_ids=true, to_apply=%region_0.0 | all-reduce | flops 786432 | bytes 4718592 | tf_op jit(solution)/shard_map/psum | solution.py:68
  194.3 1.5 copy.23
  195.9 37.6 %all-reduce.8 = (bf16[256,512]{1,0:T(8,128)(2,1)}, bf16[512,512]{1,0:T(8,128)(2,1)}) all-reduce(f32[256,512]{1,0:T(8,128)} %get-tuple-element.176, f32[512,512]{1,0:T(8,128)} %get-tuple-element.177), channel_id=1, replica_groups=mesh['row_0'=4,'row_1'=2,'col_0'=2,'col_1'=4,'col_2'=2] {'row_1'}, use_global_device_ids=true, to_apply=%region_2.0 | all-reduce | flops 393216 | bytes 2359296 | tf_op jit(solution)/shard_map/psum | solution.py:67
  233.5 127.2 %while.12 = (s32[]{:T(128)}, f32[16,512]{1,0:T(8,128)S(1)}, s32[16]{0:T(128)S(1)}, s32[16]{0:T(128)S(1)}, bf16[256,1024]{1,0:T(8,128)(2,1)}, /*index=5*/bf16[256...) while((s32[]{:T(128)}, f32[16,512]{1,0:T(8,128)S(1)}, ...), condition=%wide.region_8.9_spmd, body=%wide.region_6.8_spmd.sunk | while | flops 673316864 | bytes 5119617 | solution.py:93
  237.2 1.2 compare_and_fusion.2
  238.4 2.9 fusion.35
  245.1 1.2 compare_and_fusion.2
  246.4 2.9 fusion.35
  253.1 1.2 compare_and_fusion.2
  254.3 2.9 fusion.35
  261.0 1.2 compare_and_fusion.2
  262.3 2.9 fusion.35
  269.0 1.2 compare_and_fusion.2
  270.2 2.9 fusion.35
  278.2 2.9 fusion.35
  284.9 1.2 compare_and_fusion.2
  286.1 2.9 fusion.35
  294.1 2.9 fusion.35
  302.0 2.9 fusion.35
  310.0 2.9 fusion.35
  318.0 2.9 fusion.35
  325.9 2.9 fusion.35
  333.9 2.9 fusion.35
  341.8 2.9 fusion.35
  349.8 2.9 fusion.35
  356.5 1.2 compare_and_fusion.2
  357.7 2.9 fusion.35
  360.7 11.2 %psum.83 = f32[16,512]{1,0:T(8,128)S(1)} all-reduce(f32[16,512]{1,0:T(8,128)S(1)} %get-tuple-element.119), channel_id=1, replica_groups=mesh['row_0'=4,'row_1'=2,'col_0'=2,'col_1'=4,'col_2'=2] {'row_0'}, use_global_device_ids=true, to_apply=%region_9.10 | all-reduce | flops 8192 | bytes 65536 | tf_op jit(solution)/shard_map/psum | solution.py:36
  371.9 6.7 %psum.84 = f32[16,512]{1,0:T(8,128)S(1)} all-reduce(f32[16,512]{1,0:T(8,128)S(1)} %psum.83), channel_id=1, replica_groups=mesh['row_0'=4,'row_1'=2,'col_0'=2,'col_1'=4,'col_2'=2] {'row_1'}, use_global_device_ids=true, to_apply=%region_10.11 | all-reduce | flops 8192 | bytes 65536 | tf_op jit(solution)/shard_map/psum | solution.py:36
  378.6 5.8 %psum.85 = f32[16,512]{1,0:T(8,128)S(1)} all-reduce(f32[16,512]{1,0:T(8,128)S(1)} %psum.84), channel_id=1, replica_groups=mesh['row_0'=4,'row_1'=2,'col_0'=2,'col_1'=4,'col_2'=2] {'col_0'}, use_global_device_ids=true, to_apply=%region_11.12 | all-reduce | flops 8192 | bytes 65536 | tf_op jit(solution)/shard_map/psum | solution.py:36
  384.5 23.9 %psum.86 = f32[16,512]{1,0:T(8,128)S(1)} all-reduce(f32[16,512]{1,0:T(8,128)S(1)} %psum.85), channel_id=1, replica_groups=mesh['row_0'=4,'row_1'=2,'col_0'=2,'col_1'=4,'col_2'=2] {'col_1'}, use_global_device_ids=true, to_apply=%region_12.13 | all-reduce | flops 8192 | bytes 65536 | tf_op jit(solution)/shard_map/psum | solution.py:36
  408.3 14.8 %psum.87 = f32[16,512]{1,0:T(8,128)S(1)} all-reduce(f32[16,512]{1,0:T(8,128)S(1)} %psum.86), channel_id=1, replica_groups=mesh['row_0'=4,'row_1'=2,'col_0'=2,'col_1'=4,'col_2'=2] {'col_2'}, use_global_device_ids=true, to_apply=%region_13.14 | all-reduce | flops 8192 | bytes 65536 | tf_op jit(solution)/shard_map/psum | solution.py:36
  (89 shorter events, 39.8 us)
Async XLA Ops:
  6.5 112.3 %copy-start = (bf16[512,1024]{1,0:T(8,128)(2,1)S(1)}, bf16[512,1024]{1,0:T(8,128)(2,1)}, u32[]{:S(2)}) copy-start(bf16[512,1024]{1,0:T(8,128)(2,1)} %param.16) | copy-start | bytes 3145732
  6.5 39.5 %all-gather.4.cloned.1.call-start = ((), (), s32[]{:S(2)}) async-start(), calls=%async_computation.4 | async-start | bytes 1671168 | tf_op jit(solution)/shard_map/all_gather | solution.py:26
  22.6 28.5 %all-to-all-start = ((bf16[4,16,512]{2,0,1:T(4,128)(2,1)}), bf16[4,16,512]{2,0,1:T(4,128)(2,1)S(1)}, u32[]{:S(2)}, u32[]{:S(2)}) async-start(bf16[4,16,512]{2,0,1:T(4,128)(2,1)} %bitcast.52), calls=%async_computation | async-start | bytes 131072 | tf_op jit(solution)/shard_map/all_to_all | solution.py:57
  51.1 16.8 %all-to-all-start.2 = ((bf16[32,8,1024]{2,0,1:T(8,128)(2,1)}), bf16[32,8,1024]{2,0,1:T(8,128)(2,1)S(1)}, u32[]{:S(2)}, u32[]{:S(2)}) async-start(bf16[32,8,1024]{2,0,1:T(8,128)(2,1)} %copy.21), calls=%async_computation.2 | async-start | bytes 1048576 | tf_op jit(solution)/shard_map/all_to_all | solution.py:54
  67.9 47.7 %all-to-all-start.3 = ((bf16[64,8,1024]{2,0,1:T(8,128)(2,1)}), bf16[64,8,1024]{2,0,1:T(8,128)(2,1)}, u32[]{:S(2)}, u32[]{:S(2)}) async-start(bf16[64,8,1024]{2,0,1:T(8,128)(2,1)} %copy.22), calls=%async_computation.3 | async-start | bytes 2097152 | tf_op jit(solution)/shard_map/all_to_all | solution.py:53
  72.1 123.7 %all-reduce.7.cloned.1.call-start = ((), (), s32[]{:S(2)}) async-start(), calls=%async_computation.5 | async-start | bytes 3145728 | tf_op jit(solution)/shard_map/psum | solution.py:67
  112.1 3.5 copy-start.1
  118.9 1.8 slice-start
  194.3 39.1 %copy-start.2 = (s32[16]{0:T(128)S(1)}, s32[16]{0:T(128)}, u32[]{:S(2)}) copy-start(s32[16]{0:T(128)} %param.18) | copy-start | bytes 196
  194.3 39.1 %copy-start.3 = (s32[16]{0:T(128)S(1)}, s32[16]{0:T(128)}, u32[]{:S(2)}) copy-start(s32[16]{0:T(128)} %param.19) | copy-start | bytes 196
Sparse Core Ops, SparseCore 0:
  9.1 36.9 all-gather.3
  119.0 52.5 all-reduce.6
